TPU v7x, 256 devices: a whole 4x4x8 slice. The times are simulated.
256 devices in a mesh: seq: 128 (over z, y, x), head: 2 (over core).
Axes of the slice: x: 4, y: 4, z: 8, core: 2. Of those that a mesh axis runs over, the one named last changes fastest.
Arguments:
- queries: bfloat16 [65536, 2048], P(('seq', 'head')), may hold values from -6 to 6
- key_rows: bfloat16 [65536, 2048], P(('seq', 'head')), may hold values from -6 to 6
- values: bfloat16 [65536, 2048], P(('seq', 'head')), may hold values from -6 to 6
- out_grad: bfloat16 [65536, 2048], P(('seq', 'head')), may hold values from -6 to 6
- level_weights: float32 [16, 11], replicated, may hold values from 0.2 to 1
Outputs:
- query_grad: bfloat16 [65536, 2048], P(('seq', 'head'))
- key_grad: bfloat16 [65536, 2048], P(('seq', 'head'))
- value_grad: bfloat16 [65536, 2048], P(('seq', 'head'))
All inputs are finite; a program needn't handle non-finite values.
Results may differ from a plain program's by a relative error of at most 0.003.
Values may be sent and summed in bfloat16 or wider, within the bound.
A program may use at most 128 MiB of HBM per device.

v0:
```python
import jax
import jax.numpy as jnp
from jax import lax
from jax.sharding import PartitionSpec as P

DH = 128
BLOCK = 128


def partner(array, axis, distance):
    return lax.ppermute(array, axis, [(i, i ^ 1 << distance) for i in range(lax.axis_size(axis))])


def fenwick_local(kv_blocks, qo_blocks, level_scale):
    block_count = kv_blocks.shape[0]
    inner_shape = kv_blocks.shape[1:]
    earlier = jnp.zeros_like(kv_blocks)
    later = jnp.zeros_like(qo_blocks)
    for level_index in range(1, block_count.bit_length()):
        half_span = 1 << level_index - 1
        group_count = block_count >> level_index
        weight = level_scale[:, level_index][:, None, None]
        kv_groups = kv_blocks.reshape((group_count, 2, half_span) + inner_shape)
        qo_groups = qo_blocks.reshape((group_count, 2, half_span) + inner_shape)
        lower_sum = jnp.sum(kv_groups[:, 0], axis=1) * weight
        upper_sum = jnp.sum(qo_groups[:, 1], axis=1) * weight
        zero_block = jnp.zeros_like(lower_sum)
        add_earlier = jnp.stack([zero_block, lower_sum], axis=1)[:, :, None]
        add_later = jnp.stack([upper_sum, zero_block], axis=1)[:, :, None]
        full_shape = (group_count, 2, half_span) + inner_shape
        earlier = earlier + jnp.broadcast_to(add_earlier, full_shape).reshape(kv_blocks.shape)
        later = later + jnp.broadcast_to(add_later, full_shape).reshape(qo_blocks.shape)
    return (earlier, later)


def cross_states(kv_total, qo_total, level_scale, local_levels, swapper, position, chain_len):
    earlier = jnp.zeros_like(kv_total)
    later = jnp.zeros_like(qo_total)
    group_kv = kv_total
    group_qo = qo_total
    for bit_index in range(chain_len.bit_length() - 1):
        other_kv, other_qo = swapper((group_kv, group_qo), bit_index)
        upper_half = (position // (1 << bit_index) % 2).astype(jnp.float32)
        weight = level_scale[:, local_levels + 1 + bit_index][:, None, None]
        earlier = earlier + upper_half * weight * other_kv
        later = later + (1.0 - upper_half) * weight * other_qo
        group_kv = group_kv + other_kv
        group_qo = group_qo + other_qo
    return (earlier, later)


def range_grads(
    query_rows, key_part, value_rows, grad_rows, level_scale, swapper, position, chain_len
):
    high = lax.Precision.HIGHEST
    token_count = query_rows.shape[0]
    head_count = query_rows.shape[1] // DH
    block_count = token_count // BLOCK
    shape_four = (block_count, BLOCK, head_count, DH)
    query_blk = query_rows.reshape(shape_four)
    key_blk = key_part.reshape(shape_four)
    value_blk = value_rows.reshape(shape_four)
    grad_blk = grad_rows.reshape(shape_four)
    rows = lax.broadcasted_iota(jnp.int32, (BLOCK, BLOCK), 0)
    cols = lax.broadcasted_iota(jnp.int32, (BLOCK, BLOCK), 1)
    causal_mask = (rows >= cols).astype(jnp.float32)
    first_weight = level_scale[:, 0][None, :, None, None]
    kv_blocks = jnp.einsum(
        "nshd,nshe->nhde", key_blk, value_blk, preferred_element_type=jnp.float32
    )
    qo_blocks = jnp.einsum(
        "nthd,nthe->nhde", query_blk, grad_blk, preferred_element_type=jnp.float32
    )
    local_levels = block_count.bit_length() - 1
    earlier_dev, later_dev = cross_states(
        jnp.sum(kv_blocks, axis=0),
        jnp.sum(qo_blocks, axis=0),
        level_scale,
        local_levels,
        swapper,
        position,
        chain_len,
    )
    scores = jnp.einsum("nthd,nshd->nhts", query_blk, key_blk, preferred_element_type=jnp.float32)
    weighted = (scores * causal_mask * first_weight).astype(jnp.bfloat16)
    grad_prob = jnp.einsum(
        "nthe,nshe->nhts", grad_blk, value_blk, preferred_element_type=jnp.float32
    )
    grad_score = (grad_prob * causal_mask * first_weight).astype(jnp.bfloat16)
    value_local = jnp.einsum(
        "nhts,nthe->nshe", weighted, grad_blk, preferred_element_type=jnp.float32
    )
    query_local = jnp.einsum(
        "nhts,nshd->nthd", grad_score, key_blk, preferred_element_type=jnp.float32
    )
    key_local = jnp.einsum(
        "nhts,nthd->nshd", grad_score, query_blk, preferred_element_type=jnp.float32
    )
    earlier_local, later_local = fenwick_local(kv_blocks, qo_blocks, level_scale)
    earlier = earlier_local + earlier_dev[None]
    later = later_local + later_dev[None]
    query_cross = jnp.einsum(
        "nthe,nhde->nthd", grad_blk, earlier, precision=high, preferred_element_type=jnp.float32
    )
    key_cross = jnp.einsum(
        "nshe,nhde->nshd", value_blk, later, precision=high, preferred_element_type=jnp.float32
    )
    value_cross = jnp.einsum(
        "nshd,nhde->nshe", key_blk, later, precision=high, preferred_element_type=jnp.float32
    )
    flat_shape = (token_count, head_count * DH)
    return (
        (query_local + query_cross).astype(jnp.bfloat16).reshape(flat_shape),
        (key_local + key_cross).astype(jnp.bfloat16).reshape(flat_shape),
        (value_local + value_cross).astype(jnp.bfloat16).reshape(flat_shape),
    )


def body(queries, key_rows, values, out_grad, level_weights):
    level_ids = jnp.arange(level_weights.shape[1], dtype=jnp.float32)
    level_scale = (
        level_weights
        * jnp.exp2((1.0 - level_ids) / 2.0)[None, :]
        / jnp.sqrt(jnp.float32(DH * BLOCK))
    )
    query_rows, key_part, value_rows, grad_rows = (
        lax.all_to_all(queries, "head", split_axis=1, concat_axis=0, tiled=True),
        lax.all_to_all(key_rows, "head", split_axis=1, concat_axis=0, tiled=True),
        lax.all_to_all(values, "head", split_axis=1, concat_axis=0, tiled=True),
        lax.all_to_all(out_grad, "head", split_axis=1, concat_axis=0, tiled=True),
    )
    head_count = level_scale.shape[0] // lax.axis_size("head")
    head_scale = lax.dynamic_slice_in_dim(
        level_scale, lax.axis_index("head") * head_count, head_count, 0
    )

    def swap_heads(states, bit_index):
        return partner(states, "seq", bit_index)

    query_part, key_grad_part, value_part = range_grads(
        query_rows,
        key_part,
        value_rows,
        grad_rows,
        head_scale,
        swap_heads,
        lax.axis_index("seq"),
        lax.axis_size("seq"),
    )
    return (
        lax.all_to_all(query_part, "head", split_axis=0, concat_axis=1, tiled=True),
        lax.all_to_all(key_grad_part, "head", split_axis=0, concat_axis=1, tiled=True),
        lax.all_to_all(value_part, "head", split_axis=0, concat_axis=1, tiled=True),
    )


def solution(mesh):
    return jax.shard_map(
        body,
        mesh=mesh,
        in_specs=(
            P(("seq", "head"), None),
            P(("seq", "head"), None),
            P(("seq", "head"), None),
            P(("seq", "head"), None),
            P(),
        ),
        out_specs=(P(("seq", "head"), None), P(("seq", "head"), None), P(("seq", "head"), None)),
        check_vma=False,
    )
```

profile of v0, /device:TPU:1, one launch (start us, length us, event | category | flops | bytes accessed | tf_op | source)
XLA Modules:
  0.0 267.1 jit_solution(1590416939446828161)
XLA Ops:
  0.6 2.4 copy.180
  3.0 6.8 %all-to-all-start = ((bf16[256,2,1024]{2,0,1:T(8,128)(2,1)}), bf16[256,2,1024]{2,0,1:T(8,128)(2,1)S(1)}, u32[]{:S(2)}, u32[]{:S(2)}) async-start(bf16[256,2,1024]{2,0,1:T(8,128)(2,1)} %bitcast.96), calls=%async_computation | async-start | bytes 2097152 | tf_op jit(solution)/shard_map/all_to_all | solution.py:130
  11.6 3.9 %all-to-all-start.4 = ((bf16[256,2,1024]{2,0,1:T(8,128)(2,1)}), bf16[256,2,1024]{2,0,1:T(8,128)(2,1)S(1)}, u32[]{:S(2)}, u32[]{:S(2)}) async-start(bf16[256,2,1024]{2,0,1:T(8,128)(2,1)} %bitcast.93), calls=%async_computation.4 | async-start | bytes 2097152 | tf_op jit(solution)/shard_map/all_to_all | solution.py:127
  17.5 2.7 %fusion.31 = (f32[8,128,128]{2,1,0:T(8,128)}, f32[4,8,128,128]{3,2,1,0:T(8,128)}) fusion(bf16[4,128,8,128]{3,2,1,0:T(8,128)(2,1)S(1)} %bitcast.101, bf16[4,128,8,128]{3,2,1,0:T(8,128)(2,1)S(1)} %bitcast.105), kind=kOutput, calls=%fused_computation.72 | convolution fusion | flops 134610944 | bytes 4718592 | tf_op jit(solution)/shard_map/nthd,nthe->nhde/dot_general | solution.py:71
  21.3 3.9 %all-to-all-start.2 = ((bf16[256,2,1024]{2,0,1:T(8,128)(2,1)}), bf16[256,2,1024]{2,0,1:T(8,128)(2,1)S(1)}, u32[]{:S(2)}, u32[]{:S(2)}) async-start(bf16[256,2,1024]{2,0,1:T(8,128)(2,1)} %bitcast.119), calls=%async_computation.2 | async-start | bytes 2097152 | tf_op jit(solution)/shard_map/all_to_all | solution.py:128
  25.2 2.3 copy.179
  27.5 4.4 %all-to-all-start.1 = ((bf16[256,2,1024]{2,0,1:T(8,128)(2,1)}), bf16[256,2,1024]{2,0,1:T(8,128)(2,1)}, u32[]{:S(2)}, u32[]{:S(2)}) async-start(bf16[256,2,1024]{2,0,1:T(8,128)(2,1)} %bitcast.118), calls=%async_computation.1 | async-start | bytes 2097152 | tf_op jit(solution)/shard_map/all_to_all | solution.py:129
  35.3 2.6 fusion.30
  44.3 7.7 %collective-permute-done = f32[8,128,128]{2,1,0:T(8,128)} collective-permute-done((f32[8,128,128]{2,1,0:T(8,128)}, f32[8,128,128]{2,1,0:T(8,128)}, u32[]{:S(2)}, u32[]{:S(2)}) %collective-permute-start) | collective-permute-done | bytes 524320 | tf_op jit(solution)/shard_map/ppermute | solution.py:11
  55.0 9.0 %collective-permute-done.8 = f32[8,128,128]{2,1,0:T(8,128)} collective-permute-done((f32[8,128,128]{2,1,0:T(8,128)}, f32[8,128,128]{2,1,0:T(8,128)}, u32[]{:S(2)}, u32[]{:S(2)}) %collective-permute-start.8) | collective-permute-done | bytes 524320 | tf_op jit(solution)/shard_map/ppermute | solution.py:11
  67.2 7.9 %collective-permute-done.1 = f32[8,128,128]{2,1,0:T(8,128)S(1)} collective-permute-done((f32[8,128,128]{2,1,0:T(8,128)S(1)}, f32[8,128,128]{2,1,0:T(8,128)S(1)}, u32[]{:S(2)}, u32[]{:S(2)}) %collective-permute-start.1) | collective-permute-done | bytes 524320 | tf_op jit(solution)/shard_map/ppermute | solution.py:11
  76.8 3.0 %collective-permute-start.10 = (f32[8,128,128]{2,1,0:T(8,128)S(1)}, f32[8,128,128]{2,1,0:T(8,128)S(1)}, u32[]{:S(2)}, u32[]{:S(2)}) collective-permute-start(f32[8,128,128]{2,1,0:T(8,128)S(1)} %add.180), channel_id=1, source_target_pairs={{0,16},{2,18},{4,20},{6,22},{8,24},{10,26},{12,28},{14,30},{16,0},... | collective-permute-start | bytes 1572872 | tf_op jit(solution)/shard_map/ppermute | solution.py:11
  82.4 6.9 %collective-permute-done.2 = f32[8,128,128]{2,1,0:T(8,128)S(1)} collective-permute-done((f32[8,128,128]{2,1,0:T(8,128)S(1)}, f32[8,128,128]{2,1,0:T(8,128)S(1)}, u32[]{:S(2)}, u32[]{:S(2)}) %collective-permute-start.2) | collective-permute-done | bytes 524320 | tf_op jit(solution)/shard_map/ppermute | solution.py:11
  91.0 2.9 %collective-permute-start.3 = (f32[8,128,128]{2,1,0:T(8,128)}, f32[8,128,128]{2,1,0:T(8,128)}, u32[]{:S(2)}, u32[]{:S(2)}) collective-permute-start(f32[8,128,128]{2,1,0:T(8,128)} %add.160), channel_id=1, source_target_pairs={{0,16},{2,18},{4,20},{6,22},{8,24},{10,26},{12,28},{14,30},{16,0},... | collective-permute-start | bytes 1572872 | tf_op jit(solution)/shard_map/ppermute | solution.py:11
  93.9 9.1 %collective-permute-done.10 = f32[8,128,128]{2,1,0:T(8,128)S(1)} collective-permute-done((f32[8,128,128]{2,1,0:T(8,128)S(1)}, f32[8,128,128]{2,1,0:T(8,128)S(1)}, u32[]{:S(2)}, u32[]{:S(2)}) %collective-permute-start.10) | collective-permute-done | bytes 524320 | tf_op jit(solution)/shard_map/ppermute | solution.py:11
  107.7 2.9 %copy.102 = f32[2,2,8,128,128]{3,4,2,1,0:T(8,128)} copy(f32[2,2,8,128,128]{4,3,2,0,1:T(8,128)} %pad_add_fusion) | data formatting | bytes 4194304 | tf_op jit(solution)/shard_map/add | solution.py:32
  118.5 3.2 %collective-permute-start.12 = (f32[8,128,128]{2,1,0:T(8,128)S(1)}, f32[8,128,128]{2,1,0:T(8,128)S(1)}, u32[]{:S(2)}, u32[]{:S(2)}) collective-permute-start(f32[8,128,128]{2,1,0:T(8,128)S(1)} %add.184), channel_id=1, source_target_pairs={{0,64},{2,66},{4,68},{6,70},{8,72},{10,74},{12,76},{14,78},{16,80}... | collective-permute-start | bytes 1572872 | tf_op jit(solution)/shard_map/ppermute | solution.py:11
  124.5 12.8 %collective-permute-done.4 = f32[8,128,128]{2,1,0:T(8,128)S(1)} collective-permute-done((f32[8,128,128]{2,1,0:T(8,128)S(1)}, f32[8,128,128]{2,1,0:T(8,128)S(1)}, u32[]{:S(2)}, u32[]{:S(2)}) %collective-permute-start.4) | collective-permute-done | bytes 524320 | tf_op jit(solution)/shard_map/ppermute | solution.py:11
  142.3 5.3 %collective-permute-start.13 = (f32[8,128,128]{2,1,0:T(8,128)}, f32[8,128,128]{2,1,0:T(8,128)}, u32[]{:S(2)}, u32[]{:S(2)}) collective-permute-start(f32[8,128,128]{2,1,0:T(8,128)} %add.186), channel_id=1, source_target_pairs={{0,128},{2,130},{4,132},{6,134},{8,136},{10,138},{12,140},{14,142}... | collective-permute-start | bytes 1572872 | tf_op jit(solution)/shard_map/ppermute | solution.py:11
  149.4 2.6 fusion.3
  151.9 26.1 %collective-permute-done.5 = f32[8,128,128]{2,1,0:T(8,128)} collective-permute-done((f32[8,128,128]{2,1,0:T(8,128)}, f32[8,128,128]{2,1,0:T(8,128)}, u32[]{:S(2)}, u32[]{:S(2)}) %collective-permute-start.5) | collective-permute-done | bytes 524320 | tf_op jit(solution)/shard_map/ppermute | solution.py:11
  178.1 2.1 add.169
  180.2 13.8 %collective-permute-start.6 = (f32[8,128,128]{2,1,0:T(8,128)}, f32[8,128,128]{2,1,0:T(8,128)}, u32[]{:S(2)}, u32[]{:S(2)}) collective-permute-start(f32[8,128,128]{2,1,0:T(8,128)} %add.169), channel_id=1, source_target_pairs={{0,128},{2,130},{4,132},{6,134},{8,136},{10,138},{12,140},{14,142}... | collective-permute-start | bytes 1572872 | tf_op jit(solution)/shard_map/ppermute | solution.py:11
  194.0 2.3 multiply_add_fusion
  199.7 2.3 fusion
  204.0 33.7 %all_to_all.121 = bf16[2,256,1024]{2,1,0:T(8,128)(2,1)} all-to-all(bf16[2,256,1024]{2,1,0:T(8,128)(2,1)} %all_to_all.110), channel_id=1, replica_groups=mesh['seq'=128,'head'=2] {'head'}, dimensions={0} | all-to-all | bytes 2097152 | tf_op jit(solution)/shard_map/all_to_all | solution.py:153
  237.7 2.3 copy.116
  240.0 2.3 copy.119
  242.3 2.9 %fusion.1 = bf16[4,128,8,128]{3,1,2,0:T(8,128)(2,1)S(1)} fusion(f32[4,8,128,128]{3,2,1,0:T(8,128)} %fusion.12, f32[4,8,128,128]{2,3,1,0:T(8,128)S(1)} %bitcast_add_fusion.2, bf16[4,128,8,128]{3,2,1,0:T(8,128)(2,1)S(1)} %bitcast.110), kind=kOutput, calls=%fused_computation.3 | convolution fusion | flops 806354944 | bytes 6291456 | tf_op jit(solution)/shard_map/nshe,nhde->nshd/dot_general | solution.py:105
  246.4 4.7 %all_to_all.122 = bf16[2,256,1024]{2,1,0:T(8,128)(2,1)S(1)} all-to-all(bf16[2,256,1024]{2,1,0:T(8,128)(2,1)S(1)} %all_to_all.106), channel_id=1, replica_groups=mesh['seq'=128,'head'=2] {'head'}, dimensions={0} | all-to-all | bytes 2097152 | tf_op jit(solution)/shard_map/all_to_all | solution.py:152
  257.2 2.3 fusion.2
  260.7 4.5 %all_to_all.123 = bf16[2,256,1024]{2,1,0:T(8,128)(2,1)S(1)} all-to-all(bf16[2,256,1024]{2,1,0:T(8,128)(2,1)S(1)} %all_to_all.99), channel_id=1, replica_groups=mesh['seq'=128,'head'=2] {'head'}, dimensions={0} | all-to-all | bytes 2097152 | tf_op jit(solution)/shard_map/all_to_all | solution.py:151
  (113 shorter events, 64.4 us)
Async XLA Ops:
  0.6 9.2 %copy-start.20 = (bf16[256,2048]{1,0:T(8,128)(2,1)S(1)}, bf16[256,2048]{1,0:T(8,128)(2,1)}, u32[]{:S(2)}) copy-start(bf16[256,2048]{1,0:T(8,128)(2,1)} %param.5) | copy-start | bytes 3145732
  3.0 8.6 %all-to-all-start = ((bf16[256,2,1024]{2,0,1:T(8,128)(2,1)}), bf16[256,2,1024]{2,0,1:T(8,128)(2,1)S(1)}, u32[]{:S(2)}, u32[]{:S(2)}) async-start(bf16[256,2,1024]{2,0,1:T(8,128)(2,1)} %bitcast.96), calls=%async_computation | async-start | bytes 2097152 | tf_op jit(solution)/shard_map/all_to_all | solution.py:130
  11.6 5.7 %all-to-all-start.4 = ((bf16[256,2,1024]{2,0,1:T(8,128)(2,1)}), bf16[256,2,1024]{2,0,1:T(8,128)(2,1)S(1)}, u32[]{:S(2)}, u32[]{:S(2)}) async-start(bf16[256,2,1024]{2,0,1:T(8,128)(2,1)} %bitcast.93), calls=%async_computation.4 | async-start | bytes 2097152 | tf_op jit(solution)/shard_map/all_to_all | solution.py:127
  15.8 133.6 %copy-start = (bf16[64,8,8,128]{3,2,1,0:T(8,128)(2,1)}, bf16[64,8,8,128]{3,2,1,0:T(8,128)(2,1)S(1)}, u32[]{:S(2)}) copy-start(bf16[64,8,8,128]{3,2,1,0:T(8,128)(2,1)S(1)} %copy.131) | copy-start | bytes 3145732
  17.5 2.7 %copy-start.21 = (bf16[256,2048]{1,0:T(8,128)(2,1)S(1)}, bf16[256,2048]{1,0:T(8,128)(2,1)}, u32[]{:S(2)}) copy-start(bf16[256,2048]{1,0:T(8,128)(2,1)} %param.6) | copy-start | bytes 3145732
  20.2 19.5 %collective-permute-start.7 = (f32[8,128,128]{2,1,0:T(8,128)}, f32[8,128,128]{2,1,0:T(8,128)}, u32[]{:S(2)}, u32[]{:S(2)}) collective-permute-start(f32[8,128,128]{2,1,0:T(8,128)} %get-tuple-element.32), channel_id=1, source_target_pairs={{0,2},{2,0},{4,6},{6,4},{8,10},{10,8},{12,14},{14,12},{16,18},{18,... | collective-permute-start | bytes 1572872 | tf_op jit(solution)/shard_map/ppermute | solution.py:11
  21.3 6.2 %all-to-all-start.2 = ((bf16[256,2,1024]{2,0,1:T(8,128)(2,1)}), bf16[256,2,1024]{2,0,1:T(8,128)(2,1)S(1)}, u32[]{:S(2)}, u32[]{:S(2)}) async-start(bf16[256,2,1024]{2,0,1:T(8,128)(2,1)} %bitcast.119), calls=%async_computation.2 | async-start | bytes 2097152 | tf_op jit(solution)/shard_map/all_to_all | solution.py:128
  27.5 4.4 %copy-start.10 = (bf16[256,2,1024]{2,0,1:T(8,128)(2,1)}, bf16[256,2,1024]{2,0,1:T(8,128)(2,1)S(1)}, u32[]{:S(2)}) copy-start(bf16[256,2,1024]{2,0,1:T(8,128)(2,1)S(1)} %all-to-all-done.2) | copy-start | bytes 3145732
  27.5 6.3 %all-to-all-start.1 = ((bf16[256,2,1024]{2,0,1:T(8,128)(2,1)}), bf16[256,2,1024]{2,0,1:T(8,128)(2,1)}, u32[]{:S(2)}, u32[]{:S(2)}) async-start(bf16[256,2,1024]{2,0,1:T(8,128)(2,1)} %bitcast.118), calls=%async_computation.1 | async-start | bytes 2097152 | tf_op jit(solution)/shard_map/all_to_all | solution.py:129
  35.3 2.7 copy-start.2
  38.0 6.3 %copy-start.22 = (f32[16,11]{1,0:T(8,128)S(1)}, f32[16,11]{1,0:T(8,128)}, u32[]{:S(2)}) copy-start(f32[16,11]{1,0:T(8,128)} %param.9) | copy-start | bytes 2116
  38.0 14.1 %collective-permute-start = (f32[8,128,128]{2,1,0:T(8,128)}, f32[8,128,128]{2,1,0:T(8,128)}, u32[]{:S(2)}, u32[]{:S(2)}) collective-permute-start(f32[8,128,128]{2,1,0:T(8,128)} %get-tuple-element.30), channel_id=1, source_target_pairs={{0,2},{2,0},{4,6},{6,4},{8,10},{10,8},{12,14},{14,12},{16,18},{18,... | collective-permute-start | bytes 1572872 | tf_op jit(solution)/shard_map/ppermute | solution.py:11
  41.8 22.2 %collective-permute-start.8 = (f32[8,128,128]{2,1,0:T(8,128)}, f32[8,128,128]{2,1,0:T(8,128)}, u32[]{:S(2)}, u32[]{:S(2)}) collective-permute-start(f32[8,128,128]{2,1,0:T(8,128)} %add.176), channel_id=1, source_target_pairs={{0,4},{2,6},{4,0},{6,2},{8,12},{10,14},{12,8},{14,10},{16,20},{18,... | collective-permute-start | bytes 1572872 | tf_op jit(solution)/shard_map/ppermute | solution.py:11
  42.8 24.1 %copy-start.8 = (f32[4,8,128,128]{3,2,1,0:T(8,128)S(1)}, f32[4,8,128,128]{3,2,1,0:T(8,128)}, u32[]{:S(2)}) copy-start(f32[4,8,128,128]{3,2,1,0:T(8,128)} %get-tuple-element.31) | copy-start | bytes 6291460
  53.3 21.8 %collective-permute-start.1 = (f32[8,128,128]{2,1,0:T(8,128)S(1)}, f32[8,128,128]{2,1,0:T(8,128)S(1)}, u32[]{:S(2)}, u32[]{:S(2)}) collective-permute-start(f32[8,128,128]{2,1,0:T(8,128)S(1)} %add.154), channel_id=1, source_target_pairs={{0,4},{2,6},{4,0},{6,2},{8,12},{10,14},{12,8},{14,10},{16,20},{18,... | collective-permute-start | bytes 1572872 | tf_op jit(solution)/shard_map/ppermute | solution.py:11
  65.2 11.5 %collective-permute-start.9 = (f32[8,128,128]{2,1,0:T(8,128)S(1)}, f32[8,128,128]{2,1,0:T(8,128)S(1)}, u32[]{:S(2)}, u32[]{:S(2)}) collective-permute-start(f32[8,128,128]{2,1,0:T(8,128)S(1)} %add.178), channel_id=1, source_target_pairs={{0,8},{2,10},{4,12},{6,14},{8,0},{10,2},{12,4},{14,6},{16,24},{18,... | collective-permute-start | bytes 1572872 | tf_op jit(solution)/shard_map/ppermute | solution.py:11
  75.1 6.1 %copy-start.11 = (f32[8,128,128]{2,1,0:T(8,128)}, f32[8,128,128]{2,1,0:T(8,128)S(1)}, u32[]{:S(2)}) copy-start(f32[8,128,128]{2,1,0:T(8,128)S(1)} %collective-permute-done.1) | copy-start | bytes 1572868
  75.2 6.0 %copy-start.7 = (f32[4,8,128,128]{3,2,1,0:T(8,128)S(1)}, f32[4,8,128,128]{3,2,1,0:T(8,128)}, u32[]{:S(2)}) copy-start(f32[4,8,128,128]{3,2,1,0:T(8,128)} %get-tuple-element.33) | copy-start | bytes 6291460
  75.2 14.1 %collective-permute-start.2 = (f32[8,128,128]{2,1,0:T(8,128)S(1)}, f32[8,128,128]{2,1,0:T(8,128)S(1)}, u32[]{:S(2)}, u32[]{:S(2)}) collective-permute-start(f32[8,128,128]{2,1,0:T(8,128)S(1)} %add.157), channel_id=1, source_target_pairs={{0,8},{2,10},{4,12},{6,14},{8,0},{10,2},{12,4},{14,6},{16,24},{18,... | collective-permute-start | bytes 1572872 | tf_op jit(solution)/shard_map/ppermute | solution.py:11
  76.7 3.4 %copy-start.15 = (f32[8,128,128]{2,1,0:T(8,128)}, f32[8,128,128]{2,1,0:T(8,128)S(1)}, u32[]{:S(2)}) copy-start(f32[8,128,128]{2,1,0:T(8,128)S(1)} %collective-permute-done.9) | copy-start | bytes 1572868
  76.8 26.2 %collective-permute-start.10 = (f32[8,128,128]{2,1,0:T(8,128)S(1)}, f32[8,128,128]{2,1,0:T(8,128)S(1)}, u32[]{:S(2)}, u32[]{:S(2)}) collective-permute-start(f32[8,128,128]{2,1,0:T(8,128)S(1)} %add.180), channel_id=1, source_target_pairs={{0,16},{2,18},{4,20},{6,22},{8,24},{10,26},{12,28},{14,30},{16,0},... | collective-permute-start | bytes 1572872 | tf_op jit(solution)/shard_map/ppermute | solution.py:11
  91.0 23.3 %collective-permute-start.3 = (f32[8,128,128]{2,1,0:T(8,128)}, f32[8,128,128]{2,1,0:T(8,128)}, u32[]{:S(2)}, u32[]{:S(2)}) collective-permute-start(f32[8,128,128]{2,1,0:T(8,128)} %add.160), channel_id=1, source_target_pairs={{0,16},{2,18},{4,20},{6,22},{8,24},{10,26},{12,28},{14,30},{16,0},... | collective-permute-start | bytes 1572872 | tf_op jit(solution)/shard_map/ppermute | solution.py:11
  104.6 12.7 %collective-permute-start.11 = (f32[8,128,128]{2,1,0:T(8,128)}, f32[8,128,128]{2,1,0:T(8,128)}, u32[]{:S(2)}, u32[]{:S(2)}) collective-permute-start(f32[8,128,128]{2,1,0:T(8,128)} %add.182), channel_id=1, source_target_pairs={{0,32},{2,34},{4,36},{6,38},{8,40},{10,42},{12,44},{14,46},{16,48}... | collective-permute-start | bytes 1572872 | tf_op jit(solution)/shard_map/ppermute | solution.py:11
  113.9 7.9 %copy-start.3 = (bf16[64,8,8,128]{3,2,1,0:T(8,128)(2,1)S(1)}, bf16[64,8,8,128]{3,2,1,0:T(8,128)(2,1)}, u32[]{:S(2)}) copy-start(bf16[64,8,8,128]{3,2,1,0:T(8,128)(2,1)} %copy-done.2) | copy-start | bytes 3145732
  115.6 21.8 %collective-permute-start.4 = (f32[8,128,128]{2,1,0:T(8,128)S(1)}, f32[8,128,128]{2,1,0:T(8,128)S(1)}, u32[]{:S(2)}, u32[]{:S(2)}) collective-permute-start(f32[8,128,128]{2,1,0:T(8,128)S(1)} %add.163), channel_id=1, source_target_pairs={{0,32},{2,34},{4,36},{6,38},{8,40},{10,42},{12,44},{14,46},{16,48}... | collective-permute-start | bytes 1572872 | tf_op jit(solution)/shard_map/ppermute | solution.py:11
  118.5 22.1 %collective-permute-start.12 = (f32[8,128,128]{2,1,0:T(8,128)S(1)}, f32[8,128,128]{2,1,0:T(8,128)S(1)}, u32[]{:S(2)}, u32[]{:S(2)}) collective-permute-start(f32[8,128,128]{2,1,0:T(8,128)S(1)} %add.184), channel_id=1, source_target_pairs={{0,64},{2,66},{4,68},{6,70},{8,72},{10,74},{12,76},{14,78},{16,80}... | collective-permute-start | bytes 1572872 | tf_op jit(solution)/shard_map/ppermute | solution.py:11
  139.0 39.1 %collective-permute-start.5 = (f32[8,128,128]{2,1,0:T(8,128)}, f32[8,128,128]{2,1,0:T(8,128)}, u32[]{:S(2)}, u32[]{:S(2)}) collective-permute-start(f32[8,128,128]{2,1,0:T(8,128)} %add.166), channel_id=1, source_target_pairs={{0,64},{2,66},{4,68},{6,70},{8,72},{10,74},{12,76},{14,78},{16,80}... | collective-permute-start | bytes 1572872 | tf_op jit(solution)/shard_map/ppermute | solution.py:11
  142.3 51.7 %collective-permute-start.13 = (f32[8,128,128]{2,1,0:T(8,128)}, f32[8,128,128]{2,1,0:T(8,128)}, u32[]{:S(2)}, u32[]{:S(2)}) collective-permute-start(f32[8,128,128]{2,1,0:T(8,128)} %add.186), channel_id=1, source_target_pairs={{0,128},{2,130},{4,132},{6,134},{8,136},{10,138},{12,140},{14,142}... | collective-permute-start | bytes 1572872 | tf_op jit(solution)/shard_map/ppermute | solution.py:11
  180.2 72.9 %collective-permute-start.6 = (f32[8,128,128]{2,1,0:T(8,128)}, f32[8,128,128]{2,1,0:T(8,128)}, u32[]{:S(2)}, u32[]{:S(2)}) collective-permute-start(f32[8,128,128]{2,1,0:T(8,128)} %add.169), channel_id=1, source_target_pairs={{0,128},{2,130},{4,132},{6,134},{8,136},{10,138},{12,140},{14,142}... | collective-permute-start | bytes 1572872 | tf_op jit(solution)/shard_map/ppermute | solution.py:11
  197.3 2.4 copy-start.6
  237.7 4.6 %copy-start.4 = (bf16[64,8,8,128]{3,2,1,0:T(8,128)(2,1)S(1)}, bf16[64,8,8,128]{3,2,1,0:T(8,128)(2,1)}, u32[]{:S(2)}) copy-start(bf16[64,8,8,128]{3,2,1,0:T(8,128)(2,1)} %copy-done.2) | copy-start | bytes 3145732
  253.1 2.2 copy-start.9
  (9 other events, 11.7 us)
where the time goes:
time: 268 us; the launch traced here: 267 us
  waiting for transfers between devices  82.6 us (31%)
  starting transfers between devices  59.7 us (22%)
  blocking collectives  42.8 us (16%)
  local copies, waits for them, and re-layouts  35.1 us (13%)
  other arithmetic  26.1 us (10%)
  matrix products  19.9 us (7%)
    ppermute x14, waiting for transfers between devices, partner(): lax.ppermute(array, axis, [(i, i ^ 1 << distance) for i in range(lax.axis...  80.1 us
    ppermute x14, starting transfers between devices, partner(): lax.ppermute(array, axis, [(i, i ^ 1 << distance) for i in range(lax.axis...  40.6 us
    all_to_all x1, blocking collectives, body(): lax.all_to_all(value_part, 'head', split_axis=0, concat_axis=1, tiled=True)  33.7 us
    unnamed x53, local copies, waits for them, and re-layouts  14.1 us
    all_to_all x1, starting transfers between devices, body(): lax.all_to_all(out_grad, 'head', split_axis=1, concat_axis=0, tiled=True)  6.81 us
    add x6, other arithmetic, cross_states(): group_kv = group_kv + other_kv  6.39 us
    add x6, other arithmetic, cross_states(): group_qo = group_qo + other_qo  6.31 us
  transfers between devices with their start and end apart: 18, of which 12 were waited for; matrix products, arithmetic and copies ran while one was open for 23% of the time, Pallas kernels for 0%

commit v1 on v0

--- a/solution.py
+++ b/solution.py
@@ -149,7 +149,12 @@
     )
     return (
         lax.all_to_all(query_part, "head", split_axis=0, concat_axis=1, tiled=True),
-        lax.all_to_all(key_grad_part, "head", split_axis=0, concat_axis=1, tiled=True),
+        jnp.concatenate(
+            lax.all_to_all(
+                jnp.stack(jnp.split(key_grad_part, lax.axis_size("head"), axis=0)), "head", 0, 0
+            ),
+            axis=1,
+        ),
         lax.all_to_all(value_part, "head", split_axis=0, concat_axis=1, tiled=True),
     )
 

time: 268 us -> 268 us (level)
  blocking collectives: 42.8 us -> 9 us
  starting transfers between devices: 59.7 us -> 91.6 us
    all_to_all x2 -> x1, blocking collectives: 38.3 us -> 4.43 us  [body(): lax.all_to_all(jnp.stack(jnp.split(key_grad_part, lax.axis_size('head'),...]
    all_to_all x0 -> x1, starting transfers between devices: none -> 31.9 us  [body(): lax.all_to_all(value_part, 'head', split_axis=0, concat_axis=1, tiled=True)]
    unnamed x53 -> x55, local copies, waits for them, and re-layouts: 14.1 us -> 13.2 us
  transfers between devices with their start and end apart: 18 -> 19, of which waited for: 12 -> 12; matrix products, arithmetic and copies ran while one was open for 23% -> 23% of each run, Pallas kernels for 0% -> 0%
where the time goes in v1:
time: 268 us; the launch traced here: 267 us
  starting transfers between devices  91.6 us (34%)
  waiting for transfers between devices  82.6 us (31%)
  local copies, waits for them, and re-layouts  35.6 us (13%)
  other arithmetic  26.2 us (10%)
  matrix products  20.9 us (8%)
  blocking collectives  9 us (3%)
    ppermute x14, waiting for transfers between devices, partner(): lax.ppermute(array, axis, [(i, i ^ 1 << distance) for i in range(lax.axis...  80.1 us
    ppermute x14, starting transfers between devices, partner(): lax.ppermute(array, axis, [(i, i ^ 1 << distance) for i in range(lax.axis...  40.6 us
    all_to_all x1, starting transfers between devices, body(): lax.all_to_all(value_part, 'head', split_axis=0, concat_axis=1, tiled=True)  31.9 us
    unnamed x55, local copies, waits for them, and re-layouts  13.2 us
    all_to_all x1, starting transfers between devices, body(): lax.all_to_all(out_grad, 'head', split_axis=1, concat_axis=0, tiled=True)  6.81 us
    add x6, other arithmetic, cross_states(): group_kv = group_kv + other_kv  6.39 us
    add x6, other arithmetic, cross_states(): group_qo = group_qo + other_qo  6.31 us
  transfers between devices with their start and end apart: 19, of which 12 were waited for; matrix products, arithmetic and copies ran while one was open for 23% of the time, Pallas kernels for 0%

profile of v1, /device:TPU:1, one launch (start us, length us, event | category | flops | bytes accessed | tf_op | source)
XLA Modules:
  0.0 266.8 jit_solution(3276900026312689809)
XLA Ops:
  0.6 2.4 copy.183
  3.0 6.8 %all-to-all-start = ((bf16[256,2,1024]{2,0,1:T(8,128)(2,1)}), bf16[256,2,1024]{2,0,1:T(8,128)(2,1)S(1)}, u32[]{:S(2)}, u32[]{:S(2)}) async-start(bf16[256,2,1024]{2,0,1:T(8,128)(2,1)} %bitcast.98), calls=%async_computation | async-start | bytes 2097152 | tf_op jit(solution)/shard_map/all_to_all | solution.py:130
  11.6 3.9 %all-to-all-start.4 = ((bf16[256,2,1024]{2,0,1:T(8,128)(2,1)}), bf16[256,2,1024]{2,0,1:T(8,128)(2,1)S(1)}, u32[]{:S(2)}, u32[]{:S(2)}) async-start(bf16[256,2,1024]{2,0,1:T(8,128)(2,1)} %bitcast.95), calls=%async_computation.4 | async-start | bytes 2097152 | tf_op jit(solution)/shard_map/all_to_all | solution.py:127
  17.5 2.7 %fusion.32 = (f32[8,128,128]{2,1,0:T(8,128)}, f32[4,8,128,128]{3,2,1,0:T(8,128)}) fusion(bf16[4,128,8,128]{3,2,1,0:T(8,128)(2,1)S(1)} %bitcast.103, bf16[4,128,8,128]{3,2,1,0:T(8,128)(2,1)S(1)} %bitcast.107), kind=kOutput, calls=%fused_computation.74 | convolution fusion | flops 134610944 | bytes 4718592 | tf_op jit(solution)/shard_map/nthd,nthe->nhde/dot_general | solution.py:71
  21.3 3.9 %all-to-all-start.2 = ((bf16[256,2,1024]{2,0,1:T(8,128)(2,1)}), bf16[256,2,1024]{2,0,1:T(8,128)(2,1)S(1)}, u32[]{:S(2)}, u32[]{:S(2)}) async-start(bf16[256,2,1024]{2,0,1:T(8,128)(2,1)} %bitcast.121), calls=%async_computation.2 | async-start | bytes 2097152 | tf_op jit(solution)/shard_map/all_to_all | solution.py:128
  25.2 2.3 copy.182
  27.5 4.4 %all-to-all-start.1 = ((bf16[256,2,1024]{2,0,1:T(8,128)(2,1)}), bf16[256,2,1024]{2,0,1:T(8,128)(2,1)}, u32[]{:S(2)}, u32[]{:S(2)}) async-start(bf16[256,2,1024]{2,0,1:T(8,128)(2,1)} %bitcast.120), calls=%async_computation.1 | async-start | bytes 2097152 | tf_op jit(solution)/shard_map/all_to_all | solution.py:129
  35.3 2.6 fusion.31
  44.3 7.7 %collective-permute-done = f32[8,128,128]{2,1,0:T(8,128)} collective-permute-done((f32[8,128,128]{2,1,0:T(8,128)}, f32[8,128,128]{2,1,0:T(8,128)}, u32[]{:S(2)}, u32[]{:S(2)}) %collective-permute-start) | collective-permute-done | bytes 524320 | tf_op jit(solution)/shard_map/ppermute | solution.py:11
  55.0 9.0 %collective-permute-done.8 = f32[8,128,128]{2,1,0:T(8,128)} collective-permute-done((f32[8,128,128]{2,1,0:T(8,128)}, f32[8,128,128]{2,1,0:T(8,128)}, u32[]{:S(2)}, u32[]{:S(2)}) %collective-permute-start.8) | collective-permute-done | bytes 524320 | tf_op jit(solution)/shard_map/ppermute | solution.py:11
  67.2 7.9 %collective-permute-done.1 = f32[8,128,128]{2,1,0:T(8,128)S(1)} collective-permute-done((f32[8,128,128]{2,1,0:T(8,128)S(1)}, f32[8,128,128]{2,1,0:T(8,128)S(1)}, u32[]{:S(2)}, u32[]{:S(2)}) %collective-permute-start.1) | collective-permute-done | bytes 524320 | tf_op jit(solution)/shard_map/ppermute | solution.py:11
  76.8 3.0 %collective-permute-start.10 = (f32[8,128,128]{2,1,0:T(8,128)S(1)}, f32[8,128,128]{2,1,0:T(8,128)S(1)}, u32[]{:S(2)}, u32[]{:S(2)}) collective-permute-start(f32[8,128,128]{2,1,0:T(8,128)S(1)} %add.180), channel_id=1, source_target_pairs={{0,16},{2,18},{4,20},{6,22},{8,24},{10,26},{12,28},{14,30},{16,0},... | collective-permute-start | bytes 1572872 | tf_op jit(solution)/shard_map/ppermute | solution.py:11
  82.4 6.9 %collective-permute-done.2 = f32[8,128,128]{2,1,0:T(8,128)S(1)} collective-permute-done((f32[8,128,128]{2,1,0:T(8,128)S(1)}, f32[8,128,128]{2,1,0:T(8,128)S(1)}, u32[]{:S(2)}, u32[]{:S(2)}) %collective-permute-start.2) | collective-permute-done | bytes 524320 | tf_op jit(solution)/shard_map/ppermute | solution.py:11
  91.0 2.9 %collective-permute-start.3 = (f32[8,128,128]{2,1,0:T(8,128)}, f32[8,128,128]{2,1,0:T(8,128)}, u32[]{:S(2)}, u32[]{:S(2)}) collective-permute-start(f32[8,128,128]{2,1,0:T(8,128)} %add.160), channel_id=1, source_target_pairs={{0,16},{2,18},{4,20},{6,22},{8,24},{10,26},{12,28},{14,30},{16,0},... | collective-permute-start | bytes 1572872 | tf_op jit(solution)/shard_map/ppermute | solution.py:11
  93.9 9.1 %collective-permute-done.10 = f32[8,128,128]{2,1,0:T(8,128)S(1)} collective-permute-done((f32[8,128,128]{2,1,0:T(8,128)S(1)}, f32[8,128,128]{2,1,0:T(8,128)S(1)}, u32[]{:S(2)}, u32[]{:S(2)}) %collective-permute-start.10) | collective-permute-done | bytes 524320 | tf_op jit(solution)/shard_map/ppermute | solution.py:11
  107.7 2.9 %copy.104 = f32[2,2,8,128,128]{3,4,2,1,0:T(8,128)} copy(f32[2,2,8,128,128]{4,3,2,0,1:T(8,128)} %pad_add_fusion) | data formatting | bytes 4194304 | tf_op jit(solution)/shard_map/add | solution.py:32
  118.5 3.2 %collective-permute-start.12 = (f32[8,128,128]{2,1,0:T(8,128)S(1)}, f32[8,128,128]{2,1,0:T(8,128)S(1)}, u32[]{:S(2)}, u32[]{:S(2)}) collective-permute-start(f32[8,128,128]{2,1,0:T(8,128)S(1)} %add.184), channel_id=1, source_target_pairs={{0,64},{2,66},{4,68},{6,70},{8,72},{10,74},{12,76},{14,78},{16,80}... | collective-permute-start | bytes 1572872 | tf_op jit(solution)/shard_map/ppermute | solution.py:11
  124.5 12.8 %collective-permute-done.4 = f32[8,128,128]{2,1,0:T(8,128)S(1)} collective-permute-done((f32[8,128,128]{2,1,0:T(8,128)S(1)}, f32[8,128,128]{2,1,0:T(8,128)S(1)}, u32[]{:S(2)}, u32[]{:S(2)}) %collective-permute-start.4) | collective-permute-done | bytes 524320 | tf_op jit(solution)/shard_map/ppermute | solution.py:11
  142.3 5.3 %collective-permute-start.13 = (f32[8,128,128]{2,1,0:T(8,128)}, f32[8,128,128]{2,1,0:T(8,128)}, u32[]{:S(2)}, u32[]{:S(2)}) collective-permute-start(f32[8,128,128]{2,1,0:T(8,128)} %add.186), channel_id=1, source_target_pairs={{0,128},{2,130},{4,132},{6,134},{8,136},{10,138},{12,140},{14,142}... | collective-permute-start | bytes 1572872 | tf_op jit(solution)/shard_map/ppermute | solution.py:11
  149.4 2.6 fusion.3
  151.9 26.1 %collective-permute-done.5 = f32[8,128,128]{2,1,0:T(8,128)} collective-permute-done((f32[8,128,128]{2,1,0:T(8,128)}, f32[8,128,128]{2,1,0:T(8,128)}, u32[]{:S(2)}, u32[]{:S(2)}) %collective-permute-start.5) | collective-permute-done | bytes 524320 | tf_op jit(solution)/shard_map/ppermute | solution.py:11
  178.1 2.1 add.169
  180.2 13.8 %collective-permute-start.6 = (f32[8,128,128]{2,1,0:T(8,128)}, f32[8,128,128]{2,1,0:T(8,128)}, u32[]{:S(2)}, u32[]{:S(2)}) collective-permute-start(f32[8,128,128]{2,1,0:T(8,128)} %add.169), channel_id=1, source_target_pairs={{0,128},{2,130},{4,132},{6,134},{8,136},{10,138},{12,140},{14,142}... | collective-permute-start | bytes 1572872 | tf_op jit(solution)/shard_map/ppermute | solution.py:11
  194.0 2.3 multiply_add_fusion
  197.3 2.1 bitcast_add_fusion.2
  199.7 2.3 fusion
  203.7 2.4 all_to_all.96
  206.1 31.9 %all-to-all-start.6 = ((bf16[2,256,1024]{2,1,0:T(8,128)(2,1)}), bf16[2,256,1024]{2,1,0:T(8,128)(2,1)}, u32[]{:S(2)}, u32[]{:S(2)}) async-start(bf16[2,256,1024]{2,1,0:T(8,128)(2,1)} %all_to_all.96), calls=%async_computation.6 | async-start | bytes 2097152 | tf_op jit(solution)/shard_map/all_to_all | solution.py:158
  237.9 3.9 %fusion.1 = bf16[4,128,8,128]{3,1,2,0:T(8,128)(2,1)} fusion(f32[4,8,128,128]{3,2,1,0:T(8,128)} %fusion.12, f32[4,8,128,128]{2,3,1,0:T(8,128)S(1)} %bitcast_add_fusion.2, bf16[4,128,8,128]{3,2,1,0:T(8,128)(2,1)S(1)} %bitcast.112), kind=kOutput, calls=%fused_computation.3 | convolution fusion | flops 806354944 | bytes 6291456 | tf_op jit(solution)/shard_map/nshe,nhde->nshd/dot_general | solution.py:105
  246.2 4.4 %all_to_all.107 = bf16[2,256,1024]{2,1,0:T(8,128)(2,1)S(1)} all-to-all(bf16[2,256,1024]{2,1,0:T(8,128)(2,1)S(1)} %pad_maximum_fusion), channel_id=1, replica_groups=mesh['seq'=128,'head'=2] {'head'}, dimensions={0} | all-to-all | bytes 2097152 | tf_op jit(solution)/shard_map/all_to_all | solution.py:153
  256.8 2.3 fusion.2
  260.3 4.6 %all_to_all.108 = bf16[2,256,1024]{2,1,0:T(8,128)(2,1)S(1)} all-to-all(bf16[2,256,1024]{2,1,0:T(8,128)(2,1)S(1)} %all_to_all.88), channel_id=1, replica_groups=mesh['seq'=128,'head'=2] {'head'}, dimensions={0} | all-to-all | bytes 2097152 | tf_op jit(solution)/shard_map/all_to_all | solution.py:151
  (120 shorter events, 65.1 us)
Async XLA Ops:
  0.6 9.2 %copy-start.21 = (bf16[256,2048]{1,0:T(8,128)(2,1)S(1)}, bf16[256,2048]{1,0:T(8,128)(2,1)}, u32[]{:S(2)}) copy-start(bf16[256,2048]{1,0:T(8,128)(2,1)} %param.5) | copy-start | bytes 3145732
  3.0 8.6 %all-to-all-start = ((bf16[256,2,1024]{2,0,1:T(8,128)(2,1)}), bf16[256,2,1024]{2,0,1:T(8,128)(2,1)S(1)}, u32[]{:S(2)}, u32[]{:S(2)}) async-start(bf16[256,2,1024]{2,0,1:T(8,128)(2,1)} %bitcast.98), calls=%async_computation | async-start | bytes 2097152 | tf_op jit(solution)/shard_map/all_to_all | solution.py:130
  11.6 5.7 %all-to-all-start.4 = ((bf16[256,2,1024]{2,0,1:T(8,128)(2,1)}), bf16[256,2,1024]{2,0,1:T(8,128)(2,1)S(1)}, u32[]{:S(2)}, u32[]{:S(2)}) async-start(bf16[256,2,1024]{2,0,1:T(8,128)(2,1)} %bitcast.95), calls=%async_computation.4 | async-start | bytes 2097152 | tf_op jit(solution)/shard_map/all_to_all | solution.py:127
  15.8 133.6 %copy-start = (bf16[64,8,8,128]{3,2,1,0:T(8,128)(2,1)}, bf16[64,8,8,128]{3,2,1,0:T(8,128)(2,1)S(1)}, u32[]{:S(2)}) copy-start(bf16[64,8,8,128]{3,2,1,0:T(8,128)(2,1)S(1)} %copy.134) | copy-start | bytes 3145732
  17.5 2.7 %copy-start.22 = (bf16[256,2048]{1,0:T(8,128)(2,1)S(1)}, bf16[256,2048]{1,0:T(8,128)(2,1)}, u32[]{:S(2)}) copy-start(bf16[256,2048]{1,0:T(8,128)(2,1)} %param.6) | copy-start | bytes 3145732
  20.2 19.5 %collective-permute-start.7 = (f32[8,128,128]{2,1,0:T(8,128)}, f32[8,128,128]{2,1,0:T(8,128)}, u32[]{:S(2)}, u32[]{:S(2)}) collective-permute-start(f32[8,128,128]{2,1,0:T(8,128)} %get-tuple-element.34), channel_id=1, source_target_pairs={{0,2},{2,0},{4,6},{6,4},{8,10},{10,8},{12,14},{14,12},{16,18},{18,... | collective-permute-start | bytes 1572872 | tf_op jit(solution)/shard_map/ppermute | solution.py:11
  21.3 6.2 %all-to-all-start.2 = ((bf16[256,2,1024]{2,0,1:T(8,128)(2,1)}), bf16[256,2,1024]{2,0,1:T(8,128)(2,1)S(1)}, u32[]{:S(2)}, u32[]{:S(2)}) async-start(bf16[256,2,1024]{2,0,1:T(8,128)(2,1)} %bitcast.121), calls=%async_computation.2 | async-start | bytes 2097152 | tf_op jit(solution)/shard_map/all_to_all | solution.py:128
  27.5 4.4 %copy-start.10 = (bf16[256,2,1024]{2,0,1:T(8,128)(2,1)}, bf16[256,2,1024]{2,0,1:T(8,128)(2,1)S(1)}, u32[]{:S(2)}) copy-start(bf16[256,2,1024]{2,0,1:T(8,128)(2,1)S(1)} %all-to-all-done.2) | copy-start | bytes 3145732
  27.5 6.3 %all-to-all-start.1 = ((bf16[256,2,1024]{2,0,1:T(8,128)(2,1)}), bf16[256,2,1024]{2,0,1:T(8,128)(2,1)}, u32[]{:S(2)}, u32[]{:S(2)}) async-start(bf16[256,2,1024]{2,0,1:T(8,128)(2,1)} %bitcast.120), calls=%async_computation.1 | async-start | bytes 2097152 | tf_op jit(solution)/shard_map/all_to_all | solution.py:129
  35.3 2.7 copy-start.2
  38.0 6.3 %copy-start.23 = (f32[16,11]{1,0:T(8,128)S(1)}, f32[16,11]{1,0:T(8,128)}, u32[]{:S(2)}) copy-start(f32[16,11]{1,0:T(8,128)} %param.9) | copy-start | bytes 2116
  38.0 14.1 %collective-permute-start = (f32[8,128,128]{2,1,0:T(8,128)}, f32[8,128,128]{2,1,0:T(8,128)}, u32[]{:S(2)}, u32[]{:S(2)}) collective-permute-start(f32[8,128,128]{2,1,0:T(8,128)} %get-tuple-element.32), channel_id=1, source_target_pairs={{0,2},{2,0},{4,6},{6,4},{8,10},{10,8},{12,14},{14,12},{16,18},{18,... | collective-permute-start | bytes 1572872 | tf_op jit(solution)/shard_map/ppermute | solution.py:11
  41.8 22.2 %collective-permute-start.8 = (f32[8,128,128]{2,1,0:T(8,128)}, f32[8,128,128]{2,1,0:T(8,128)}, u32[]{:S(2)}, u32[]{:S(2)}) collective-permute-start(f32[8,128,128]{2,1,0:T(8,128)} %add.176), channel_id=1, source_target_pairs={{0,4},{2,6},{4,0},{6,2},{8,12},{10,14},{12,8},{14,10},{16,20},{18,... | collective-permute-start | bytes 1572872 | tf_op jit(solution)/shard_map/ppermute | solution.py:11
  42.8 24.1 %copy-start.8 = (f32[4,8,128,128]{3,2,1,0:T(8,128)S(1)}, f32[4,8,128,128]{3,2,1,0:T(8,128)}, u32[]{:S(2)}) copy-start(f32[4,8,128,128]{3,2,1,0:T(8,128)} %get-tuple-element.33) | copy-start | bytes 6291460
  53.3 21.8 %collective-permute-start.1 = (f32[8,128,128]{2,1,0:T(8,128)S(1)}, f32[8,128,128]{2,1,0:T(8,128)S(1)}, u32[]{:S(2)}, u32[]{:S(2)}) collective-permute-start(f32[8,128,128]{2,1,0:T(8,128)S(1)} %add.154), channel_id=1, source_target_pairs={{0,4},{2,6},{4,0},{6,2},{8,12},{10,14},{12,8},{14,10},{16,20},{18,... | collective-permute-start | bytes 1572872 | tf_op jit(solution)/shard_map/ppermute | solution.py:11
  65.2 11.5 %collective-permute-start.9 = (f32[8,128,128]{2,1,0:T(8,128)S(1)}, f32[8,128,128]{2,1,0:T(8,128)S(1)}, u32[]{:S(2)}, u32[]{:S(2)}) collective-permute-start(f32[8,128,128]{2,1,0:T(8,128)S(1)} %add.178), channel_id=1, source_target_pairs={{0,8},{2,10},{4,12},{6,14},{8,0},{10,2},{12,4},{14,6},{16,24},{18,... | collective-permute-start | bytes 1572872 | tf_op jit(solution)/shard_map/ppermute | solution.py:11
  75.1 6.1 %copy-start.12 = (f32[8,128,128]{2,1,0:T(8,128)}, f32[8,128,128]{2,1,0:T(8,128)S(1)}, u32[]{:S(2)}) copy-start(f32[8,128,128]{2,1,0:T(8,128)S(1)} %collective-permute-done.1) | copy-start | bytes 1572868
  75.2 6.0 %copy-start.7 = (f32[4,8,128,128]{3,2,1,0:T(8,128)S(1)}, f32[4,8,128,128]{3,2,1,0:T(8,128)}, u32[]{:S(2)}) copy-start(f32[4,8,128,128]{3,2,1,0:T(8,128)} %get-tuple-element.35) | copy-start | bytes 6291460
  75.2 14.1 %collective-permute-start.2 = (f32[8,128,128]{2,1,0:T(8,128)S(1)}, f32[8,128,128]{2,1,0:T(8,128)S(1)}, u32[]{:S(2)}, u32[]{:S(2)}) collective-permute-start(f32[8,128,128]{2,1,0:T(8,128)S(1)} %add.157), channel_id=1, source_target_pairs={{0,8},{2,10},{4,12},{6,14},{8,0},{10,2},{12,4},{14,6},{16,24},{18,... | collective-permute-start | bytes 1572872 | tf_op jit(solution)/shard_map/ppermute | solution.py:11
  76.7 3.4 %copy-start.16 = (f32[8,128,128]{2,1,0:T(8,128)}, f32[8,128,128]{2,1,0:T(8,128)S(1)}, u32[]{:S(2)}) copy-start(f32[8,128,128]{2,1,0:T(8,128)S(1)} %collective-permute-done.9) | copy-start | bytes 1572868
  76.8 26.2 %collective-permute-start.10 = (f32[8,128,128]{2,1,0:T(8,128)S(1)}, f32[8,128,128]{2,1,0:T(8,128)S(1)}, u32[]{:S(2)}, u32[]{:S(2)}) collective-permute-start(f32[8,128,128]{2,1,0:T(8,128)S(1)} %add.180), channel_id=1, source_target_pairs={{0,16},{2,18},{4,20},{6,22},{8,24},{10,26},{12,28},{14,30},{16,0},... | collective-permute-start | bytes 1572872 | tf_op jit(solution)/shard_map/ppermute | solution.py:11
  91.0 23.3 %collective-permute-start.3 = (f32[8,128,128]{2,1,0:T(8,128)}, f32[8,128,128]{2,1,0:T(8,128)}, u32[]{:S(2)}, u32[]{:S(2)}) collective-permute-start(f32[8,128,128]{2,1,0:T(8,128)} %add.160), channel_id=1, source_target_pairs={{0,16},{2,18},{4,20},{6,22},{8,24},{10,26},{12,28},{14,30},{16,0},... | collective-permute-start | bytes 1572872 | tf_op jit(solution)/shard_map/ppermute | solution.py:11
  104.6 12.7 %collective-permute-start.11 = (f32[8,128,128]{2,1,0:T(8,128)}, f32[8,128,128]{2,1,0:T(8,128)}, u32[]{:S(2)}, u32[]{:S(2)}) collective-permute-start(f32[8,128,128]{2,1,0:T(8,128)} %add.182), channel_id=1, source_target_pairs={{0,32},{2,34},{4,36},{6,38},{8,40},{10,42},{12,44},{14,46},{16,48}... | collective-permute-start | bytes 1572872 | tf_op jit(solution)/shard_map/ppermute | solution.py:11
  113.9 7.9 %copy-start.3 = (bf16[64,8,8,128]{3,2,1,0:T(8,128)(2,1)S(1)}, bf16[64,8,8,128]{3,2,1,0:T(8,128)(2,1)}, u32[]{:S(2)}) copy-start(bf16[64,8,8,128]{3,2,1,0:T(8,128)(2,1)} %copy-done.2) | copy-start | bytes 3145732
  115.6 21.8 %collective-permute-start.4 = (f32[8,128,128]{2,1,0:T(8,128)S(1)}, f32[8,128,128]{2,1,0:T(8,128)S(1)}, u32[]{:S(2)}, u32[]{:S(2)}) collective-permute-start(f32[8,128,128]{2,1,0:T(8,128)S(1)} %add.163), channel_id=1, source_target_pairs={{0,32},{2,34},{4,36},{6,38},{8,40},{10,42},{12,44},{14,46},{16,48}... | collective-permute-start | bytes 1572872 | tf_op jit(solution)/shard_map/ppermute | solution.py:11
  118.5 22.1 %collective-permute-start.12 = (f32[8,128,128]{2,1,0:T(8,128)S(1)}, f32[8,128,128]{2,1,0:T(8,128)S(1)}, u32[]{:S(2)}, u32[]{:S(2)}) collective-permute-start(f32[8,128,128]{2,1,0:T(8,128)S(1)} %add.184), channel_id=1, source_target_pairs={{0,64},{2,66},{4,68},{6,70},{8,72},{10,74},{12,76},{14,78},{16,80}... | collective-permute-start | bytes 1572872 | tf_op jit(solution)/shard_map/ppermute | solution.py:11
  139.0 39.1 %collective-permute-start.5 = (f32[8,128,128]{2,1,0:T(8,128)}, f32[8,128,128]{2,1,0:T(8,128)}, u32[]{:S(2)}, u32[]{:S(2)}) collective-permute-start(f32[8,128,128]{2,1,0:T(8,128)} %add.166), channel_id=1, source_target_pairs={{0,64},{2,66},{4,68},{6,70},{8,72},{10,74},{12,76},{14,78},{16,80}... | collective-permute-start | bytes 1572872 | tf_op jit(solution)/shard_map/ppermute | solution.py:11
  142.3 51.7 %collective-permute-start.13 = (f32[8,128,128]{2,1,0:T(8,128)}, f32[8,128,128]{2,1,0:T(8,128)}, u32[]{:S(2)}, u32[]{:S(2)}) collective-permute-start(f32[8,128,128]{2,1,0:T(8,128)} %add.186), channel_id=1, source_target_pairs={{0,128},{2,130},{4,132},{6,134},{8,136},{10,138},{12,140},{14,142}... | collective-permute-start | bytes 1572872 | tf_op jit(solution)/shard_map/ppermute | solution.py:11
  180.2 72.5 %collective-permute-start.6 = (f32[8,128,128]{2,1,0:T(8,128)}, f32[8,128,128]{2,1,0:T(8,128)}, u32[]{:S(2)}, u32[]{:S(2)}) collective-permute-start(f32[8,128,128]{2,1,0:T(8,128)} %add.169), channel_id=1, source_target_pairs={{0,128},{2,130},{4,132},{6,134},{8,136},{10,138},{12,140},{14,142}... | collective-permute-start | bytes 1572872 | tf_op jit(solution)/shard_map/ppermute | solution.py:11
  203.7 34.2 %copy-start.4 = (bf16[64,8,8,128]{3,2,1,0:T(8,128)(2,1)S(1)}, bf16[64,8,8,128]{3,2,1,0:T(8,128)(2,1)}, u32[]{:S(2)}) copy-start(bf16[64,8,8,128]{3,2,1,0:T(8,128)(2,1)} %copy-done.2) | copy-start | bytes 3145732
  206.1 35.8 %all-to-all-start.6 = ((bf16[2,256,1024]{2,1,0:T(8,128)(2,1)}), bf16[2,256,1024]{2,1,0:T(8,128)(2,1)}, u32[]{:S(2)}, u32[]{:S(2)}) async-start(bf16[2,256,1024]{2,1,0:T(8,128)(2,1)} %all_to_all.96), calls=%async_computation.6 | async-start | bytes 2097152 | tf_op jit(solution)/shard_map/all_to_all | solution.py:158
  241.8 3.0 %copy-start.11 = (bf16[4,128,8,128]{3,1,2,0:T(8,128)(2,1)S(1)}, bf16[4,128,8,128]{3,1,2,0:T(8,128)(2,1)}, u32[]{:S(2)}) copy-start(bf16[4,128,8,128]{3,1,2,0:T(8,128)(2,1)} %fusion.1) | copy-start | bytes 3145732
  (11 other events, 16.3 us)
